TPU v7x, 32 devices: a whole 2x2x4 slice. The times are simulated.
32 devices in a mesh: ctx: 16 (over z, x, core), head: 2 (over y).
Axes of the slice: x: 2, y: 2, z: 4, core: 2. Of those that a mesh axis runs over, the one named last changes fastest.
Arguments:
- queries: bfloat16 [64, 2048], P(('ctx', 'head')), may hold values from -150 to 150
- new_block_keys: bfloat16 [64, 512], P(('ctx', 'head')), may hold values from -6 to 6
- new_block_values: bfloat16 [64, 512], P(('ctx', 'head')), may hold values from -6 to 6
- stored_keys: bfloat16 [7168, 512], P('ctx', 'head'), may hold values from -6 to 6
- stored_values: bfloat16 [7168, 512], P('ctx', 'head'), may hold values from -6 to 6
- stretch_start: int32 [1], replicated, may hold values from 3584 to 7168
- block_order: int32 [32], replicated, may hold values from 0 to 31, each once
Outputs:
- attended: bfloat16 [64, 2048], P(('ctx', 'head'))
Inputs may be any that keep to these rules, and one draw needn't show every extreme that they name: `block_order`: each value appears once.
All inputs are finite; a program needn't handle non-finite values.
Results may differ from a plain program's by a relative error of at most 0.0049.
Values may be sent and summed in bfloat16 or wider, within the bound.
A program may use at most 128 MiB of HBM per device.

v0:
```python
import math
import jax
import jax.numpy as jnp
from jax import lax
from jax.sharding import PartitionSpec as P

QUERY_HEADS = 16
KEY_VALUE_HEADS = 4
HEAD_WIDTH = 128
NEG_FILL = -1e30


def on_device(
    queries,
    new_block_keys,
    new_block_values,
    stored_keys,
    stored_values,
    stretch_start,
    block_order,
):
    local_query, local_keys, local_values = (
        lax.all_to_all(queries, "head", split_axis=1, concat_axis=0, tiled=True),
        lax.all_to_all(new_block_keys, "head", split_axis=1, concat_axis=0, tiled=True),
        lax.all_to_all(new_block_values, "head", split_axis=1, concat_axis=0, tiled=True),
    )
    query_rows = local_keys.shape[0]
    cache_rows = stored_keys.shape[0]
    kv_width = local_keys.shape[1]
    kv_heads = kv_width // HEAD_WIDTH
    query_group_width = QUERY_HEADS // KEY_VALUE_HEADS
    half_rows = query_rows // 2
    stretch_first = stretch_start[0]
    context = lax.axis_index("ctx")
    fresh_rows = context * query_rows + jnp.arange(query_rows, dtype=jnp.int32)
    fresh_pos = (
        stretch_first + block_order[fresh_rows // half_rows] * half_rows + fresh_rows % half_rows
    )
    cache_pos = context * cache_rows + jnp.arange(cache_rows, dtype=jnp.int32)
    key_pos = jnp.concatenate([fresh_pos, cache_pos])
    usable = jnp.concatenate([jnp.ones((query_rows,), dtype=bool), cache_pos < stretch_first])
    key_count = query_rows + cache_rows
    key_rows = jnp.concatenate([local_keys, stored_keys], axis=0).reshape(
        key_count, kv_heads, HEAD_WIDTH
    )
    value_rows = jnp.concatenate([local_values, stored_values], axis=0).reshape(
        key_count, kv_heads, HEAD_WIDTH
    )
    score_scale = 1.0 / math.sqrt(HEAD_WIDTH)
    piece = lax.all_gather(local_query, "ctx", axis=0, tiled=True)
    piece_rows = piece.shape[0]
    grouped = piece.reshape(piece_rows, kv_heads, query_group_width, HEAD_WIDTH)
    scores = (
        jnp.einsum("qhgd,khd->qhgk", grouped, key_rows, preferred_element_type=jnp.float32)
        * score_scale
    )
    row_index = jnp.arange(piece_rows, dtype=jnp.int32)
    query_pos = (
        stretch_first + block_order[row_index // half_rows] * half_rows + row_index % half_rows
    )
    allowed = usable[None, :] & (key_pos[None, :] <= query_pos[:, None])
    scores = jnp.where(allowed[:, None, None, :], scores, NEG_FILL)
    stretch_rows = scores.shape[0]
    peaks = lax.pmax(jnp.max(scores, axis=-1), "ctx")
    block_len = math.gcd(stretch_rows, 512)
    block_count = stretch_rows // block_len
    score_blocks = scores.reshape(block_count, block_len, kv_heads, query_group_width, key_count)
    peak_blocks = peaks.reshape(block_count, block_len, kv_heads, query_group_width)

    def weigh_block(inputs):
        block_scores, block_peaks = inputs
        weights = jnp.exp(block_scores - block_peaks[..., None])
        totals = jnp.sum(weights, axis=-1)
        product = jnp.einsum(
            "qhgk,khd->qhgd",
            weights.astype(jnp.bfloat16),
            value_rows,
            preferred_element_type=jnp.float32,
        )
        return (
            product.reshape(block_len, kv_heads * query_group_width * HEAD_WIDTH),
            totals.reshape(block_len, kv_heads * query_group_width),
        )

    sum_blocks, total_blocks = lax.map(weigh_block, (score_blocks, peak_blocks))
    weighted = sum_blocks.reshape(stretch_rows, kv_heads * query_group_width * HEAD_WIDTH)
    totals_all = total_blocks.reshape(stretch_rows, kv_heads * query_group_width)
    part_sums, part_totals = (
        lax.psum_scatter(weighted, "ctx", scatter_dimension=0, tiled=True),
        lax.psum_scatter(totals_all, "ctx", scatter_dimension=0, tiled=True),
    )
    own_rows = part_sums.shape[0]
    result = (
        part_sums.reshape(own_rows, kv_heads * query_group_width, HEAD_WIDTH)
        / part_totals[..., None]
    )
    result = result.reshape(own_rows, kv_heads * query_group_width * HEAD_WIDTH).astype(
        jnp.bfloat16
    )
    return lax.all_to_all(result, "head", split_axis=0, concat_axis=1, tiled=True)


def solution(mesh):
    return jax.shard_map(
        on_device,
        mesh=mesh,
        in_specs=(
            P(("ctx", "head"), None),
            P(("ctx", "head"), None),
            P(("ctx", "head"), None),
            P("ctx", "head"),
            P("ctx", "head"),
            P(),
            P(),
        ),
        out_specs=P(("ctx", "head"), None),
        check_vma=False,
    )
```

profile of v0, /device:TPU:0, one launch (start us, length us, event | category | flops | bytes accessed | tf_op | source)
XLA Modules:
  0.0 212.5 jit_solution(3873993751585935543)
XLA Ops:
  6.5 4.4 %all-to-all-start.1 = ((bf16[2,2,256]{2,0,1:T(2,128)(2,1)}), bf16[2,2,256]{2,0,1:T(2,128)(2,1)S(1)}, u32[]{:S(2)}, u32[]{:S(2)}) async-start(bf16[2,2,256]{2,0,1:T(2,128)(2,1)} %bitcast.60), calls=%async_computation.1 | async-start | bytes 4096 | tf_op jit(solution)/shard_map/all_to_all | solution.py:24
  11.6 0.6 copy-done.1
  12.3 0.6 gather_fusion
  12.9 0.8 gather_fusion.1
  13.7 0.9 copy-done.2
  14.7 0.1 pad_add_fusion
  14.7 3.3 %all-to-all-start = ((bf16[2,2,256]{2,0,1:T(2,128)(2,1)}), bf16[2,2,256]{2,0,1:T(2,128)(2,1)S(1)}, u32[]{:S(2)}, u32[]{:S(2)}) async-start(bf16[2,2,256]{2,0,1:T(2,128)(2,1)} %bitcast), calls=%async_computation | async-start | bytes 4096 | tf_op jit(solution)/shard_map/all_to_all | solution.py:25
  18.0 0.1 concatenate.25
  18.1 3.7 %all-to-all-done = bf16[2,2,256]{2,0,1:T(2,128)(2,1)S(1)} async-done(((bf16[2,2,256]{2,0,1:T(2,128)(2,1)}), bf16[2,2,256]{2,0,1:T(2,128)(2,1)S(1)}, u32[]{:S(2)}, u32[]{:S(2)}) %all-to-all-start) | async-done | bytes 2080 | tf_op jit(solution)/shard_map/all_to_all | solution.py:25
  21.8 3.2 %all-to-all-start.2 = ((bf16[2,2,1024]{2,0,1:T(2,128)(2,1)}), bf16[2,2,1024]{2,0,1:T(2,128)(2,1)S(1)}, u32[]{:S(2)}, u32[]{:S(2)}) async-start(bf16[2,2,1024]{2,0,1:T(2,128)(2,1)} %bitcast.11), calls=%async_computation.2 | async-start | bytes 16384 | tf_op jit(solution)/shard_map/all_to_all | solution.py:23
  25.1 0.0 all-reduce.5.cloned.1.call-start
  25.1 0.1 compare_and_fusion
  25.2 0.6 copy-done.3
  25.9 0.6 dynamic-slice.2
  27.1 1.7 all-to-all-done.2
  28.9 22.4 %all-gather = bf16[16,4,1024]{2,1,0:T(4,128)(2,1)S(1)} all-gather(bf16[1,4,1024]{2,1,0:T(4,128)(2,1)S(1)} %reshape.221), channel_id=1, replica_groups=mesh['ctx'=16,'head'=2] {'ctx'}, dimensions={0}, use_global_device_ids=true | all-gather | bytes 139264 | tf_op jit(solution)/shard_map/all_gather | solution.py:50
  51.2 0.1 reshape.202
  51.3 0.4 fusion.19
  51.7 29.8 %pmax.7 = f32[64,2,4]{0,2,1:T(4,128)S(1)} all-reduce(f32[64,2,4]{0,2,1:T(4,128)S(1)} %get-tuple-element.15), channel_id=1, replica_groups=mesh['ctx'=16,'head'=2] {'ctx'}, use_global_device_ids=true, to_apply=%region_1.2 | all-reduce | flops 512 | bytes 4096 | tf_op jit(solution)/shard_map/pmax | solution.py:64
  81.5 0.3 fusion.2
  81.9 29.5 %all-reduce.2 = f32[64,8]{0,1:T(8,128)S(1)} all-reduce(f32[64,8]{0,1:T(8,128)S(1)} %bitcast.57), channel_id=3, replica_groups=mesh['ctx'=16,'head'=2] {'ctx'}, use_global_device_ids=true, to_apply=%region_4.5.clone | all-reduce | flops 512 | bytes 4096
  111.4 0.1 constant_dynamic-slice_fusion
  111.5 0.1 copy.27
  111.5 0.4 convolution_bitcast_fusion
  111.9 0.2 copy.26
  112.1 0.8 reshape.203
  112.9 0.0 all-reduce.5.cloned.1.call-update
  112.9 0.1 broadcast_bitcast_fusion
  113.0 84.9 %all-reduce.5.cloned.1.call-done = f32[64,1024]{1,0:T(8,128)} async-done(((f32[64,1024]{1,0:T(8,128)}), f32[64,1024]{1,0:T(8,128)}) %all-reduce.5.cloned.1.call-update) | async-done | bytes 262160
  197.9 0.8 fusion.11
  198.7 6.4 %all_to_all.70 = bf16[2,2,1024]{2,1,0:T(2,128)(2,1)S(1)} all-to-all(bf16[2,2,1024]{2,1,0:T(2,128)(2,1)S(1)} %all_to_all.62), channel_id=1, replica_groups=mesh['ctx'=16,'head'=2] {'head'}, dimensions={0} | all-to-all | bytes 16384 | tf_op jit(solution)/shard_map/all_to_all | solution.py:100
  205.0 0.6 copy.47
  (22 shorter events, 0.2 us)
Async XLA Ops:
  6.5 7.1 %copy-start = (bf16[448,256]{1,0:T(8,128)(2,1)S(1)}, bf16[448,256]{1,0:T(8,128)(2,1)}, u32[]{:S(2)}) copy-start(bf16[448,256]{1,0:T(8,128)(2,1)} %param.10) | copy-start | bytes 688132
  6.5 8.2 %all-to-all-start.1 = ((bf16[2,2,256]{2,0,1:T(2,128)(2,1)}), bf16[2,2,256]{2,0,1:T(2,128)(2,1)S(1)}, u32[]{:S(2)}, u32[]{:S(2)}) async-start(bf16[2,2,256]{2,0,1:T(2,128)(2,1)} %bitcast.60), calls=%async_computation.1 | async-start | bytes 4096 | tf_op jit(solution)/shard_map/all_to_all | solution.py:24
  11.6 0.7 copy-start.1
  13.7 0.9 copy-start.2
  14.7 7.1 %all-to-all-start = ((bf16[2,2,256]{2,0,1:T(2,128)(2,1)}), bf16[2,2,256]{2,0,1:T(2,128)(2,1)S(1)}, u32[]{:S(2)}, u32[]{:S(2)}) async-start(bf16[2,2,256]{2,0,1:T(2,128)(2,1)} %bitcast), calls=%async_computation | async-start | bytes 4096 | tf_op jit(solution)/shard_map/all_to_all | solution.py:25
  21.8 7.0 %all-to-all-start.2 = ((bf16[2,2,1024]{2,0,1:T(2,128)(2,1)}), bf16[2,2,1024]{2,0,1:T(2,128)(2,1)S(1)}, u32[]{:S(2)}, u32[]{:S(2)}) async-start(bf16[2,2,1024]{2,0,1:T(2,128)(2,1)} %bitcast.11), calls=%async_computation.2 | async-start | bytes 16384 | tf_op jit(solution)/shard_map/all_to_all | solution.py:23
  25.1 172.8 %all-reduce.5.cloned.1.call-start = ((), (), s32[]{:S(2)}) async-start(), calls=%async_computation.4 | async-start | bytes 524288
  25.2 0.7 copy-start.3
Sparse Core Ops, SparseCore 0:
  113.0 84.7 all-reduce.4
where the time goes:
time: 213 us; the launch traced here: 212 us
  waiting for transfers between devices  90.3 us (42%)
  blocking collectives  88.1 us (41%)
  between operations  14.8 us (7%)
  starting transfers between devices  10.9 us (5%)
  local copies, waits for them, and re-layouts  6.24 us (3%)
    unnamed x2, waiting for transfers between devices  84.9 us
    pmax x1, blocking collectives, on_device(): peaks = lax.pmax(jnp.max(scores, axis=-1), 'ctx')  29.8 us
    unnamed x1, blocking collectives  29.5 us
    all_gather x1, blocking collectives, on_device(): piece = lax.all_gather(local_query, 'ctx', axis=0, tiled=True)  22.4 us
    all_to_all x1, blocking collectives, on_device(): lax.all_to_all(result, 'head', split_axis=0, concat_axis=1, tiled=True)  6.36 us
    all_to_all x1, starting transfers between devices, on_device(): lax.all_to_all(new_block_keys, 'head', split_axis=1, concat_axis=0, tiled...  4.37 us
  transfers between devices with their start and end apart: 4, of which 3 were waited for; matrix products, arithmetic and copies ran while one was open for 1% of the time, Pallas kernels for 0%

commit v1 on v0

--- a/solution.py
+++ b/solution.py
@@ -8,6 +8,25 @@
 KEY_VALUE_HEADS = 4
 HEAD_WIDTH = 128
 NEG_FILL = -1e30
+
+
+def in_order(pieces, dim):
+    dims = list(pieces.shape[1:])
+    dims[dim] *= pieces.shape[0]
+    return jnp.moveaxis(pieces, 0, dim).reshape(dims)
+
+
+def collected_by_bits(x, axis):
+    count, index = (lax.axis_size(axis), lax.axis_index(axis))
+    blocks, bit = (x[None], 1)
+    while bit < count:
+        received = lax.ppermute(blocks, axis, [(i, i ^ bit) for i in range(count)])
+        low = index & bit == 0
+        blocks = jnp.concatenate(
+            [jnp.where(low, blocks, received), jnp.where(low, received, blocks)]
+        )
+        bit *= 2
+    return blocks
 
 
 def on_device(
@@ -47,7 +66,7 @@
         key_count, kv_heads, HEAD_WIDTH
     )
     score_scale = 1.0 / math.sqrt(HEAD_WIDTH)
-    piece = lax.all_gather(local_query, "ctx", axis=0, tiled=True)
+    piece = in_order(collected_by_bits(local_query, "ctx"), 0)
     piece_rows = piece.shape[0]
     grouped = piece.reshape(piece_rows, kv_heads, query_group_width, HEAD_WIDTH)
     scores = (

time: 213 us -> 199 us (0.934)
  blocking collectives: 88.1 us -> 65.3 us
  starting transfers between devices: 10.9 us -> 18.1 us
  waiting for transfers between devices: 90.3 us -> 92.8 us
    all_gather x1 -> x0, blocking collectives: 22.4 us -> none  [on_device(): piece = lax.all_gather(local_query, 'ctx', axis=0, tiled=True)]
    ppermute x0 -> x4, starting transfers between devices: none -> 7.21 us  [collected_by_bits(): received = lax.ppermute(blocks, axis, [(i, i ^ bit) for i in range(count)])]
    ppermute x0 -> x4, waiting for transfers between devices: none -> 4.71 us  [collected_by_bits(): received = lax.ppermute(blocks, axis, [(i, i ^ bit) for i in range(count)])]
  transfers between devices with their start and end apart: 4 -> 8, of which waited for: 3 -> 6; matrix products, arithmetic and copies ran while one was open for 1% -> 1% of each run, Pallas kernels for 0% -> 0%
where the time goes in v1:
time: 199 us; the launch traced here: 198 us
  waiting for transfers between devices  92.8 us (47%)
  blocking collectives  65.3 us (33%)
  starting transfers between devices  18.1 us (9%)
  between operations  14.9 us (7%)
  local copies, waits for them, and re-layouts  4.86 us (2%)
    unnamed x2, waiting for transfers between devices  84.9 us
    pmax x1, blocking collectives, on_device(): peaks = lax.pmax(jnp.max(scores, axis=-1), 'ctx')  29.5 us
    unnamed x1, blocking collectives  29.5 us
    ppermute x4, starting transfers between devices, collected_by_bits(): received = lax.ppermute(blocks, axis, [(i, i ^ bit) for i in range(count)])  7.21 us
    all_to_all x1, blocking collectives, on_device(): lax.all_to_all(result, 'head', split_axis=0, concat_axis=1, tiled=True)  6.36 us
    ppermute x4, waiting for transfers between devices, collected_by_bits(): received = lax.ppermute(blocks, axis, [(i, i ^ bit) for i in range(count)])  4.71 us
    all_to_all x1, starting transfers between devices, on_device(): lax.all_to_all(queries, 'head', split_axis=1, concat_axis=0, tiled=True)  4.37 us
  transfers between devices with their start and end apart: 8, of which 6 were waited for; matrix products, arithmetic and copies ran while one was open for 1% of the time, Pallas kernels for 0%

profile of v1, /device:TPU:0, one launch (start us, length us, event | category | flops | bytes accessed | tf_op | source)
XLA Modules:
  0.0 198.4 jit_solution(7553657963574069180)
XLA Ops:
  6.5 4.4 %all-to-all-start.2 = ((bf16[2,2,1024]{2,0,1:T(2,128)(2,1)}), bf16[2,2,1024]{2,0,1:T(2,128)(2,1)S(1)}, u32[]{:S(2)}, u32[]{:S(2)}) async-start(bf16[2,2,1024]{2,0,1:T(2,128)(2,1)} %bitcast.58), calls=%async_computation.2 | async-start | bytes 16384 | tf_op jit(solution)/shard_map/all_to_all | solution.py:42
  11.7 0.6 gather_fusion
  12.3 0.8 gather_fusion.1
  13.1 0.2 copy-done.2
  13.3 1.4 all-to-all-done.2
  14.7 3.2 %all-to-all-start.1 = ((bf16[2,2,256]{2,0,1:T(2,128)(2,1)}), bf16[2,2,256]{2,0,1:T(2,128)(2,1)S(1)}, u32[]{:S(2)}, u32[]{:S(2)}) async-start(bf16[2,2,256]{2,0,1:T(2,128)(2,1)} %bitcast.7), calls=%async_computation.1 | async-start | bytes 4096 | tf_op jit(solution)/shard_map/all_to_all | solution.py:43
  18.1 1.1 collective-permute-done
  19.2 2.0 %collective-permute-start.1 = (bf16[2,4,1024]{2,1,0:T(4,128)(2,1)S(1)}, bf16[2,4,1024]{2,1,0:T(4,128)(2,1)S(1)}, u32[]{:S(2)}, u32[]{:S(2)}) collective-permute-start(bf16[2,4,1024]{2,1,0:T(4,128)(2,1)S(1)} %pad_maximum_fusion.3), channel_id=1, source_target_pairs={{0,4},{2,6},{4,0},{6,2},{8,12},{10,14},{12,8},{14,10},{16,20},{18,... | collective-permute-start | bytes 49160 | tf_op jit(solution)/shard_map/ppermute | solution.py:23
  21.3 1.7 collective-permute-done.1
  23.1 2.1 %collective-permute-start.2 = (bf16[4,4,1024]{2,1,0:T(4,128)(2,1)S(1)}, bf16[4,4,1024]{2,1,0:T(4,128)(2,1)S(1)}, u32[]{:S(2)}, u32[]{:S(2)}) collective-permute-start(bf16[4,4,1024]{2,1,0:T(4,128)(2,1)S(1)} %pad_maximum_fusion.2), channel_id=1, source_target_pairs={{0,8},{2,10},{4,12},{6,14},{8,0},{10,2},{12,4},{14,6},{16,24},{18,... | collective-permute-start | bytes 98312 | tf_op jit(solution)/shard_map/ppermute | solution.py:23
  25.2 0.1 concatenate.37
  25.3 1.8 collective-permute-done.2
  27.2 3.1 %collective-permute-start.3 = (bf16[8,4,1024]{2,1,0:T(4,128)(2,1)S(1)}, bf16[8,4,1024]{2,1,0:T(4,128)(2,1)S(1)}, u32[]{:S(2)}, u32[]{:S(2)}) collective-permute-start(bf16[8,4,1024]{2,1,0:T(4,128)(2,1)S(1)} %pad_maximum_fusion.1), channel_id=1, source_target_pairs={{0,16},{2,18},{4,20},{6,22},{8,24},{10,26},{12,28},{14,30},{16,0},... | collective-permute-start | bytes 196616 | tf_op jit(solution)/shard_map/ppermute | solution.py:23
  30.3 3.2 %all-to-all-start = ((bf16[2,2,256]{2,0,1:T(2,128)(2,1)}), bf16[2,2,256]{2,0,1:T(2,128)(2,1)S(1)}, u32[]{:S(2)}, u32[]{:S(2)}) async-start(bf16[2,2,256]{2,0,1:T(2,128)(2,1)} %bitcast), calls=%async_computation | async-start | bytes 4096 | tf_op jit(solution)/shard_map/all_to_all | solution.py:44
  33.6 0.1 compare_and_fusion
  33.7 0.6 copy-done.3
  34.3 0.6 dynamic-slice.2
  35.6 1.7 all-to-all-done
  37.3 0.1 broadcast_select_fusion.1
  37.4 0.1 pad_maximum_fusion
  37.5 0.4 fusion.19
  37.9 29.5 %pmax.7 = f32[64,2,4]{0,2,1:T(4,128)S(1)} all-reduce(f32[64,2,4]{0,2,1:T(4,128)S(1)} %get-tuple-element.31), channel_id=1, replica_groups=mesh['ctx'=16,'head'=2] {'ctx'}, use_global_device_ids=true, to_apply=%region_1.2 | all-reduce | flops 512 | bytes 4096 | tf_op jit(solution)/shard_map/pmax | solution.py:83
  67.4 0.3 fusion.2
  67.8 29.5 %all-reduce.2 = f32[64,8]{0,1:T(8,128)S(1)} all-reduce(f32[64,8]{0,1:T(8,128)S(1)} %bitcast.57), channel_id=3, replica_groups=mesh['ctx'=16,'head'=2] {'ctx'}, use_global_device_ids=true, to_apply=%region_4.5.clone | all-reduce | flops 512 | bytes 4096
  97.4 0.1 copy.27
  97.4 0.4 convolution_bitcast_fusion
  97.8 0.2 copy.26
  98.0 0.8 reshape.200
  98.9 84.9 %all-reduce.5.cloned.1.call-done = f32[64,1024]{1,0:T(8,128)} async-done(((f32[64,1024]{1,0:T(8,128)}), f32[64,1024]{1,0:T(8,128)}) %all-reduce.5.cloned.1.call-update) | async-done | bytes 262160
  183.8 0.8 fusion.11
  184.6 6.4 %all_to_all.67 = bf16[2,2,1024]{2,1,0:T(2,128)(2,1)S(1)} all-to-all(bf16[2,2,1024]{2,1,0:T(2,128)(2,1)S(1)} %all_to_all.59), channel_id=1, replica_groups=mesh['ctx'=16,'head'=2] {'head'}, dimensions={0} | all-to-all | bytes 16384 | tf_op jit(solution)/shard_map/all_to_all | solution.py:119
  190.9 0.6 copy.47
  (37 shorter events, 0.8 us)
Async XLA Ops:
  6.5 4.4 %copy-start = (bf16[448,256]{1,0:T(8,128)(2,1)S(1)}, bf16[448,256]{1,0:T(8,128)(2,1)}, u32[]{:S(2)}) copy-start(bf16[448,256]{1,0:T(8,128)(2,1)} %param.10) | copy-start | bytes 688132
  6.5 8.2 %all-to-all-start.2 = ((bf16[2,2,1024]{2,0,1:T(2,128)(2,1)}), bf16[2,2,1024]{2,0,1:T(2,128)(2,1)S(1)}, u32[]{:S(2)}, u32[]{:S(2)}) async-start(bf16[2,2,1024]{2,0,1:T(2,128)(2,1)} %bitcast.58), calls=%async_computation.2 | async-start | bytes 16384 | tf_op jit(solution)/shard_map/all_to_all | solution.py:42
  11.0 0.7 copy-start.1
  12.3 0.9 copy-start.2
  14.7 15.6 %all-to-all-start.1 = ((bf16[2,2,256]{2,0,1:T(2,128)(2,1)}), bf16[2,2,256]{2,0,1:T(2,128)(2,1)S(1)}, u32[]{:S(2)}, u32[]{:S(2)}) async-start(bf16[2,2,256]{2,0,1:T(2,128)(2,1)} %bitcast.7), calls=%async_computation.1 | async-start | bytes 4096 | tf_op jit(solution)/shard_map/all_to_all | solution.py:43
  18.0 1.2 collective-permute-start
  19.2 3.8 %collective-permute-start.1 = (bf16[2,4,1024]{2,1,0:T(4,128)(2,1)S(1)}, bf16[2,4,1024]{2,1,0:T(4,128)(2,1)S(1)}, u32[]{:S(2)}, u32[]{:S(2)}) collective-permute-start(bf16[2,4,1024]{2,1,0:T(4,128)(2,1)S(1)} %pad_maximum_fusion.3), channel_id=1, source_target_pairs={{0,4},{2,6},{4,0},{6,2},{8,12},{10,14},{12,8},{14,10},{16,20},{18,... | collective-permute-start | bytes 49160 | tf_op jit(solution)/shard_map/ppermute | solution.py:23
  23.1 4.0 %collective-permute-start.2 = (bf16[4,4,1024]{2,1,0:T(4,128)(2,1)S(1)}, bf16[4,4,1024]{2,1,0:T(4,128)(2,1)S(1)}, u32[]{:S(2)}, u32[]{:S(2)}) collective-permute-start(bf16[4,4,1024]{2,1,0:T(4,128)(2,1)S(1)} %pad_maximum_fusion.2), channel_id=1, source_target_pairs={{0,8},{2,10},{4,12},{6,14},{8,0},{10,2},{12,4},{14,6},{16,24},{18,... | collective-permute-start | bytes 98312 | tf_op jit(solution)/shard_map/ppermute | solution.py:23
  27.2 10.1 %collective-permute-start.3 = (bf16[8,4,1024]{2,1,0:T(4,128)(2,1)S(1)}, bf16[8,4,1024]{2,1,0:T(4,128)(2,1)S(1)}, u32[]{:S(2)}, u32[]{:S(2)}) collective-permute-start(bf16[8,4,1024]{2,1,0:T(4,128)(2,1)S(1)} %pad_maximum_fusion.1), channel_id=1, source_target_pairs={{0,16},{2,18},{4,20},{6,22},{8,24},{10,26},{12,28},{14,30},{16,0},... | collective-permute-start | bytes 196616 | tf_op jit(solution)/shard_map/ppermute | solution.py:23
  30.3 7.0 %all-to-all-start = ((bf16[2,2,256]{2,0,1:T(2,128)(2,1)}), bf16[2,2,256]{2,0,1:T(2,128)(2,1)S(1)}, u32[]{:S(2)}, u32[]{:S(2)}) async-start(bf16[2,2,256]{2,0,1:T(2,128)(2,1)} %bitcast), calls=%async_computation | async-start | bytes 4096 | tf_op jit(solution)/shard_map/all_to_all | solution.py:44
  33.5 150.3 %all-reduce.5.cloned.1.call-start = ((), (), s32[]{:S(2)}) async-start(), calls=%async_computation.4 | async-start | bytes 524288
  33.7 0.7 copy-start.3
Sparse Core Ops, SparseCore 0:
  98.9 84.8 all-reduce.4
